TPU v7x, 32 devices: a whole 2x2x4 slice. The times are simulated.
32 devices in a mesh: dp: 8 (over y, x, core), tensor: 4 (over z).
Axes of the slice: x: 2, y: 2, z: 4, core: 2. Of those that a mesh axis runs over, the one named last changes fastest.
Arguments:
- hidden: bfloat16 [8192, 1536], P('dp'), may hold values from -6 to 6
- norm_gain: float32 [1536], replicated, may hold values from 0.25 to 1.75
- zx_proj: bfloat16 [1536, 2, 3072], P(None, None, 'tensor'), may hold values from -0.15625 to 0.15625
- bc_proj: bfloat16 [1536, 256], replicated, may hold values from -0.15625 to 0.15625
- dt_proj: bfloat16 [1536, 48], P(None, 'tensor'), may hold values from -0.15625 to 0.15625
- conv_x: float32 [5, 3072], P(None, 'tensor'), may hold values from -3 to 3
- conv_bc: float32 [5, 256], replicated, may hold values from -3 to 3
- dt_bias: float32 [48], P('tensor'), may hold values from -7 to -3
- a_log: float32 [48], P('tensor'), may hold values from -4 to 0.5
- d_skip: float32 [48], P('tensor'), may hold values from 0.5 to 1.5
- gate_gain: float32 [3072], P('tensor'), may hold values from 0.25 to 1.75
- out_proj: bfloat16 [1536, 3072], P(None, 'tensor'), may hold values from -0.109375 to 0.109375
- cotangent: bfloat16 [8192, 1536], P('dp'), may hold values from -6 to 6
Outputs:
- block_out: bfloat16 [8192, 1536], P('dp')
- grad_hidden: bfloat16 [8192, 1536], P('dp')
- grad_norm_gain: float32 [1536], replicated
- grad_zx_proj: float32 [1536, 2, 3072], P('dp', None, 'tensor')
- grad_bc_proj: float32 [1536, 256], P('dp')
- grad_dt_proj: float32 [1536, 48], P('dp', 'tensor')
- grad_conv_x: float32 [5, 3072], P(None, 'tensor')
- grad_conv_bc: float32 [5, 256], replicated
- grad_dt_bias: float32 [48], P('tensor')
- grad_a_log: float32 [48], P('tensor')
- grad_d_skip: float32 [48], P('tensor')
- grad_gate_gain: float32 [3072], P('tensor')
- grad_out_proj: float32 [1536, 3072], P('dp', 'tensor')
All inputs are finite; a program needn't handle non-finite values.
Results may differ from a plain program's by a relative error of at most 0.005.
The roundings to bfloat16 on the way count: a program that leaves them out, or rounds other values in their place, can miss the bound.
Values may be sent and summed in bfloat16 or wider, within the bound.
No kernel may reach another device: no remote copies, remote signals or barrier semaphores. Data moves between devices by JAX's collectives and lax.ppermute only.
A program may use at most 192 MiB of HBM per device.

v0:
```python
import jax
import jax.numpy as jnp
from jax import lax
from jax.sharding import PartitionSpec as P

KCONV = 4
BLOCK_LEN = 256
SEQ_DEVS = 8


EPSILON = 1e-05
PRECISE = lax.Precision.HIGHEST


def shifted(x, axis, by):
    length = lax.axis_size(axis)
    pairs = [(i, i + by) for i in range(length) if 0 <= i + by < length]
    return lax.ppermute(x, axis, pairs)


def swish_value(operand):
    return operand * jax.nn.sigmoid(operand)


def swish_slope(operand):
    logistic = jax.nn.sigmoid(operand)
    return logistic * (1.0 + operand * (1.0 - logistic))


def product_nt(first_op, second_op):
    return lax.dot_general(
        first_op, second_op, (((1,), (1,)), ((), ())), preferred_element_type=jnp.float32
    )


def product_tn(first_op, second_op):
    return lax.dot_general(
        first_op, second_op, (((0,), (0,)), ((), ())), preferred_element_type=jnp.float32
    )


def shards(
    hidden,
    norm_gain,
    zx_proj,
    bc_proj,
    dt_proj,
    conv_x,
    conv_bc,
    dt_bias,
    a_log,
    d_skip,
    gate_gain,
    out_proj,
    cotangent,
):
    tokens = hidden.shape[0]
    model_width = hidden.shape[1]
    inner_local = zx_proj.shape[2]
    heads_local = dt_proj.shape[1]
    head_size = inner_local // heads_local
    state_size = bc_proj.shape[1] // 2
    inner_total = inner_local * lax.axis_size("tensor")
    blocks = tokens // BLOCK_LEN
    position = lax.axis_index("dp") % SEQ_DEVS
    opens_seq = position == 0
    closes_seq = position == SEQ_DEVS - 1
    residual = hidden.astype(jnp.float32)
    inv_rms = lax.rsqrt(jnp.mean(residual * residual, axis=1, keepdims=True) + EPSILON)
    normed = residual * inv_rms
    normed_low = (normed * norm_gain).astype(jnp.bfloat16)
    zx_flat = zx_proj.reshape(model_width, 2 * inner_local)
    zx_out = jnp.dot(normed_low, zx_flat, preferred_element_type=jnp.float32)
    gate_low = zx_out[:, :inner_local].astype(jnp.bfloat16)
    bc_out = jnp.dot(normed_low, bc_proj, preferred_element_type=jnp.float32)
    dt_raw = jnp.dot(normed_low, dt_proj, preferred_element_type=jnp.float32)
    conv_in = jnp.concatenate(
        [zx_out[:, inner_local:].astype(jnp.bfloat16), bc_out.astype(jnp.bfloat16)], axis=1
    )
    conv_weights = jnp.concatenate([conv_x, conv_bc], axis=1)
    rim_rows = shifted(conv_in[tokens - (KCONV - 1) :], "dp", 1)
    rim_rows = jnp.where(opens_seq, jnp.zeros_like(rim_rows), rim_rows)
    padded = jnp.concatenate([rim_rows, conv_in], axis=0).astype(jnp.float32)
    conv_pre = conv_weights[KCONV] + conv_weights[0] * padded[0:tokens]
    for tap_index in range(1, KCONV):
        conv_pre = conv_pre + conv_weights[tap_index] * padded[tap_index : tap_index + tokens]
    conv_act = swish_value(conv_pre)
    inputs = conv_act[:, :inner_local].reshape(blocks, BLOCK_LEN, heads_local, head_size)
    b_rows = conv_act[:, inner_local : inner_local + state_size].reshape(
        blocks, BLOCK_LEN, state_size
    )
    c_rows = conv_act[:, inner_local + state_size :].reshape(blocks, BLOCK_LEN, state_size)
    dt_pre = dt_raw + dt_bias
    step_size = jax.nn.softplus(dt_pre)
    decay_rate = -jnp.exp(a_log)
    step_blocks = step_size.reshape(blocks, BLOCK_LEN, heads_local)
    cumulative = jnp.cumsum(
        (decay_rate * step_size).reshape(blocks, BLOCK_LEN, heads_local), axis=1
    )
    cumul_heads = jnp.swapaxes(cumulative, 1, 2)
    step_heads = jnp.swapaxes(step_blocks, 1, 2)
    row_index = lax.broadcasted_iota(jnp.int32, (BLOCK_LEN, BLOCK_LEN), 0)
    col_index = lax.broadcasted_iota(jnp.int32, (BLOCK_LEN, BLOCK_LEN), 1)
    within = (row_index >= col_index)[None, None, :, :]
    spread = cumul_heads[:, :, :, None] - cumul_heads[:, :, None, :]
    decay_pairs = jnp.where(within, jnp.exp(jnp.where(within, spread, 0.0)), 0.0)
    affinity = jnp.einsum("kin,kjn->kij", c_rows, b_rows, precision=PRECISE)
    pair_weight = decay_pairs * step_heads[:, :, None, :]
    mixing = affinity[:, None, :, :] * pair_weight
    intra_out = jnp.einsum("khij,kjhp->kihp", mixing, inputs, precision=PRECISE)
    end_exp = jnp.exp(cumulative[:, -1:, :] - cumulative)
    to_end = end_exp * step_blocks
    sent_state = jnp.einsum("kjhp,kjn->khpn", to_end[..., None] * inputs, b_rows, precision=PRECISE)
    block_decay = jnp.exp(cumulative[:, -1, :])
    zero_state = jnp.zeros((heads_local, head_size, state_size), jnp.float32)
    local_in = [zero_state]
    decay_before = [jnp.ones((heads_local,), jnp.float32)]
    for block_index in range(blocks):
        local_in.append(
            block_decay[block_index][:, None, None] * local_in[-1] + sent_state[block_index]
        )
        decay_before.append(decay_before[-1] * block_decay[block_index])
    own_state = local_in[blocks]
    own_decay = decay_before[blocks]
    entry_decay = jnp.where(opens_seq, 0.0, own_decay)

    def relay_state(turn_index, incoming):
        return shifted(entry_decay[:, None, None] * incoming + own_state, "dp", 1)

    arrived = lax.fori_loop(0, SEQ_DEVS - 1, relay_state, jnp.zeros_like(own_state))
    arrived = jnp.where(opens_seq, 0.0, arrived)
    states_in = (
        jnp.stack(local_in[:blocks]) + jnp.stack(decay_before[:blocks])[:, :, None, None] * arrived
    )
    exp_cumul = jnp.exp(cumulative)
    inter_out = exp_cumul[..., None] * jnp.einsum(
        "kin,khpn->kihp", c_rows, states_in, precision=PRECISE
    )
    ssd_out = intra_out + inter_out + d_skip[:, None] * inputs
    ssd_flat = ssd_out.reshape(tokens, inner_local)
    gate_wide = gate_low.astype(jnp.float32)
    gate_act = swish_value(gate_wide)
    gated_out = ssd_flat * gate_act
    gated_low = (gated_out * gate_gain).astype(jnp.bfloat16)
    partial_proj = product_nt(gated_low, out_proj)
    proj_sum, square_sum = lax.psum(
        (partial_proj, jnp.sum(gated_out * gated_out, axis=1)), "tensor"
    )
    inv_gate = lax.rsqrt(square_sum / inner_total + EPSILON)[:, None]
    block_out = (residual + inv_gate * proj_sum).astype(jnp.bfloat16)
    grad_top = cotangent.astype(jnp.float32)
    grad_proj = (inv_gate * grad_top).astype(jnp.bfloat16)
    grad_inv = jnp.sum(grad_top * proj_sum, axis=1, keepdims=True)
    grad_gated_low = jnp.dot(grad_proj, out_proj, preferred_element_type=jnp.float32)
    grad_out_local = product_tn(grad_proj, gated_low)
    grad_gate_gain = jnp.sum(grad_gated_low * gated_out, axis=0)
    grad_gated = (
        grad_gated_low * gate_gain
        - grad_inv * inv_gate * inv_gate * inv_gate / inner_total * gated_out
    )
    grad_ssd = (grad_gated * gate_act).reshape(blocks, BLOCK_LEN, heads_local, head_size)
    grad_gate = (grad_gated * ssd_flat * swish_slope(gate_wide)).astype(jnp.bfloat16)
    grad_skip = jnp.sum(grad_ssd * inputs, axis=(0, 1, 3))
    grad_scaled = grad_ssd * exp_cumul[..., None]
    grad_c = jnp.einsum("kihp,khpn->kin", grad_scaled, states_in, precision=PRECISE)
    grad_from_out = jnp.einsum("kihp,kin->khpn", grad_scaled, c_rows, precision=PRECISE)
    grad_cumul = jnp.sum(grad_ssd * inter_out, axis=3)
    grad_mixing = jnp.einsum("kihp,kjhp->khij", grad_ssd, inputs, precision=PRECISE)
    grad_inputs = d_skip[:, None] * grad_ssd + jnp.einsum(
        "khij,kihp->kjhp", mixing, grad_ssd, precision=PRECISE
    )
    grad_affinity = jnp.sum(grad_mixing * pair_weight, axis=1)
    grad_pairs = grad_mixing * affinity[:, None, :, :] * decay_pairs
    grad_step = jnp.swapaxes(jnp.sum(grad_pairs, axis=2), 1, 2)
    grad_spread = grad_pairs * step_heads[:, :, None, :]
    grad_cumul = grad_cumul + jnp.swapaxes(
        jnp.sum(grad_spread, axis=3) - jnp.sum(grad_spread, axis=2), 1, 2
    )
    grad_c = grad_c + jnp.einsum("kij,kjn->kin", grad_affinity, b_rows, precision=PRECISE)
    grad_b = jnp.einsum("kij,kin->kjn", grad_affinity, c_rows, precision=PRECISE)
    local_grad = [zero_state]
    decay_after = [jnp.ones((heads_local,), jnp.float32)]
    for block_index in reversed(range(blocks)):
        local_grad.insert(
            0, grad_from_out[block_index] + block_decay[block_index][:, None, None] * local_grad[0]
        )
        decay_after.insert(0, decay_after[0] * block_decay[block_index])
    own_grad = local_grad[0]
    exit_decay = jnp.where(closes_seq, 0.0, own_decay)

    def relay_grad(turn_index, incoming):
        return shifted(exit_decay[:, None, None] * incoming + own_grad, "dp", -1)

    back_arrived = lax.fori_loop(0, SEQ_DEVS - 1, relay_grad, jnp.zeros_like(own_grad))
    back_arrived = jnp.where(closes_seq, 0.0, back_arrived)
    grad_states = jnp.stack(local_grad) + jnp.stack(decay_after)[:, :, None, None] * back_arrived
    grad_send = grad_states[1:]
    state_back = jnp.einsum("khpn,kjn->kjhp", grad_send, b_rows, precision=PRECISE)
    grad_to_end = jnp.sum(inputs * state_back, axis=3)
    grad_inputs = grad_inputs + to_end[..., None] * state_back
    grad_b = grad_b + jnp.einsum(
        "kjhp,khpn->kjn", to_end[..., None] * inputs, grad_send, precision=PRECISE
    )
    grad_step = grad_step + grad_to_end * end_exp
    weighted = grad_to_end * to_end
    grad_last = jnp.sum(weighted, axis=1) + block_decay * jnp.sum(
        grad_send * states_in, axis=(2, 3)
    )
    grad_cumul = (grad_cumul - weighted).at[:, -1, :].add(grad_last)
    grad_log = jnp.flip(jnp.cumsum(jnp.flip(grad_cumul, 1), axis=1), 1).reshape(tokens, heads_local)
    grad_a_log = decay_rate * jnp.sum(grad_log * step_size, axis=0)
    grad_dt_pre = (grad_step.reshape(tokens, heads_local) + decay_rate * grad_log) * jax.nn.sigmoid(
        dt_pre
    )
    grad_dt_bias = jnp.sum(grad_dt_pre, axis=0)
    grad_dt_low = grad_dt_pre.astype(jnp.bfloat16)
    grad_bc_act = lax.psum(
        jnp.concatenate([grad_b, grad_c], axis=2).reshape(tokens, 2 * state_size), "tensor"
    )
    grad_act = jnp.concatenate([grad_inputs.reshape(tokens, inner_local), grad_bc_act], axis=1)
    grad_pre = grad_act * swish_slope(conv_pre)
    rim_back = shifted(grad_pre[: KCONV - 1], "dp", -1)
    rim_back = jnp.where(closes_seq, 0.0, rim_back)
    extended = jnp.concatenate([grad_pre, rim_back], axis=0)
    grad_conv_in = conv_weights[0] * extended[KCONV - 1 : KCONV - 1 + tokens]
    for tap_index in range(1, KCONV):
        grad_conv_in = (
            grad_conv_in
            + conv_weights[tap_index]
            * extended[KCONV - 1 - tap_index : KCONV - 1 - tap_index + tokens]
        )
    grad_taps = jnp.stack(
        [
            jnp.sum(grad_pre * padded[tap_index : tap_index + tokens], axis=0)
            for tap_index in range(KCONV)
        ]
        + [jnp.sum(grad_pre, axis=0)]
    )
    grad_inner_low = grad_conv_in[:, :inner_local].astype(jnp.bfloat16)
    grad_bc_low = grad_conv_in[:, inner_local:].astype(jnp.bfloat16)
    grad_zx_low = jnp.concatenate([grad_gate, grad_inner_low], axis=1)
    grad_normed_part = product_nt(grad_zx_low, zx_flat) + product_nt(grad_dt_low, dt_proj)
    grad_normed = lax.psum(grad_normed_part, "tensor") + product_nt(grad_bc_low, bc_proj)
    grad_norm_local = jnp.sum(grad_normed * normed, axis=0)
    grad_scaled_in = grad_normed * norm_gain
    grad_resid = inv_rms * (
        grad_scaled_in - normed * jnp.mean(grad_scaled_in * normed, axis=1, keepdims=True)
    )
    grad_hidden = (grad_top + grad_resid).astype(jnp.bfloat16)
    grad_zx_local = product_tn(normed_low, grad_zx_low).reshape(model_width, 2, inner_local)
    grad_bc_local = product_tn(normed_low, grad_bc_low)
    grad_dt_local = product_tn(normed_low, grad_dt_low)
    grad_zx_proj, grad_bc_proj, grad_dt_proj, grad_out_proj = (
        lax.psum_scatter(grad_zx_local, "dp", scatter_dimension=0, tiled=True),
        lax.psum_scatter(grad_bc_local, "dp", scatter_dimension=0, tiled=True),
        lax.psum_scatter(grad_dt_local, "dp", scatter_dimension=0, tiled=True),
        lax.psum_scatter(grad_out_local, "dp", scatter_dimension=0, tiled=True),
    )
    (
        grad_norm_gain,
        grad_conv_x,
        grad_conv_bc,
        grad_dt_bias,
        grad_a_log,
        grad_d_skip,
        grad_gate_gain,
    ) = lax.psum(
        (
            grad_norm_local,
            grad_taps[:, :inner_local],
            grad_taps[:, inner_local:],
            grad_dt_bias,
            grad_a_log,
            grad_skip,
            grad_gate_gain,
        ),
        "dp",
    )
    return (
        block_out,
        grad_hidden,
        grad_norm_gain,
        grad_zx_proj,
        grad_bc_proj,
        grad_dt_proj,
        grad_conv_x,
        grad_conv_bc,
        grad_dt_bias,
        grad_a_log,
        grad_d_skip,
        grad_gate_gain,
        grad_out_proj,
    )


def solution(mesh):
    in_specs = (
        P("dp", None),
        P(),
        P(None, None, "tensor"),
        P(),
        P(None, "tensor"),
        P(None, "tensor"),
        P(),
        P("tensor"),
        P("tensor"),
        P("tensor"),
        P("tensor"),
        P(None, "tensor"),
        P("dp", None),
    )
    out_specs = (
        P("dp", None),
        P("dp", None),
        P(),
        P("dp", None, "tensor"),
        P("dp", None),
        P("dp", "tensor"),
        P(None, "tensor"),
        P(),
        P("tensor"),
        P("tensor"),
        P("tensor"),
        P("tensor"),
        P("dp", "tensor"),
    )
    return jax.shard_map(shards, mesh=mesh, in_specs=in_specs, out_specs=out_specs, check_vma=False)
```

profile of v0, /device:TPU:0, one launch (start us, length us, event | category | flops | bytes accessed | tf_op | source)
XLA Modules:
  0.0 1144.8 jit_solution(1173458592556442112)
XLA Ops:
  15.6 5.2 convolution_convert_fusion
  46.4 4.0 fusion.41
  58.0 5.1 reshape.184
  63.2 5.0 fusion.57
  69.6 59.2 %while.21 = (s32[]{:T(128)}, f32[12,64,128]{2,1,0:T(8,128)S(1)}, f32[12]{0:T(128)S(1)}, f32[12,64,128]{2,1,0:T(8,128)S(1)}, s32[]{:T(128)}) while((s32[]{:T(128)}, f32[12,64,128]{2,1,0:T(8,128)S(1)}, f32[12]{0:T(128)S(1)}, f32[12,64,128]{2,1,0:T(8,128)S(1)}, s32[]{:T(128)}) %tuple.107), condition=%wide.region_4.5_spmd, body=%wide.region_3.4_spmd.sunk | while | flops 196610 | bytes 2752661 | solution.py:130
  69.8 4.6 collective-permute-start
  75.8 5.3 collective-permute-start
  82.6 7.8 collective-permute-start
  91.8 7.8 collective-permute-start
  101.0 7.8 collective-permute-start
  110.2 7.8 collective-permute-start
  119.4 7.8 collective-permute-start
  134.9 15.0 %fusion.50 = f32[4,256,12,64]{1,3,2,0:T(8,128)S(1)} fusion(f32[4,256,12,64]{1,3,2,0:T(8,128)S(1)} %fusion.134, f32[4,256,12,64]{1,0,3,2:T(4,128)S(1)} %copy-done.4, f32[4,12,256]{2,1,0:T(8,128)S(1)} %copy-done.59, f32[4,12,256]{2,1,0:T(8,128)S(1)} %copy-done.58, f32[4,256,256]{2,1,0:T(8,128)S(1)} %fusion.141, pred[256,256]{1,0:T(8,128)(4,1)S(1)} %copy-done.61, ...), kind=kOutput, calls=%fused_computation.80 | convolution fusion | flops 2434793472 | bytes 10698800 | tf_op jit(solution)/shard_map/khij,kjhp->kihp/dot_general | solution.py:110
  163.2 4.6 fusion.100
  168.5 12.0 %psum.77 = f32[1024]{0:T(1024)S(1)} all-reduce(f32[1024]{0:T(1024)S(1)} %get-tuple-element.116), channel_id=1, replica_groups=mesh['dp'=8,'tensor'=4] {'tensor'}, use_global_device_ids=true, to_apply=%region_6.7 | all-reduce | flops 1024 | bytes 8192 | tf_op jit(solution)/shard_map/psum | solution.py:146
  180.6 223.6 %all-reduce.7.cloned.1.call-done = f32[1024,1536]{1,0:T(8,128)} async-done(((f32[1024,1536]{1,0:T(8,128)}), f32[1024,1536]{1,0:T(8,128)}) %all-reduce.7.cloned.1.call-update) | async-done | bytes 6291472 | tf_op jit(solution)/shard_map/psum | solution.py:146
  404.2 7.0 fusion.18
  413.9 7.6 multiply_reduce_fusion.8
  425.1 5.2 reshape.192
  430.4 5.0 fusion.53
  436.7 65.4 %while.22 = (s32[]{:T(128)}, f32[12,64,128]{2,1,0:T(8,128)S(1)}, f32[12]{0:T(128)S(1)}, f32[12,64,128]{2,1,0:T(8,128)S(1)}, s32[]{:T(128)}) while((s32[]{:T(128)}, f32[12,64,128]{2,1,0:T(8,128)S(1)}, f32[12]{0:T(128)S(1)}, f32[12,64,128]{2,1,0:T(8,128)S(1)}, s32[]{:T(128)}) %tuple.106), condition=%wide.region_10.11_spmd, body=%wide.region_9.10_spmd.sunk | while | flops 196610 | bytes 2752661 | solution.py:194
  443.6 7.3 collective-permute-done.1
  453.1 8.0 collective-permute-done.1
  463.2 8.0 collective-permute-done.1
  473.4 8.0 collective-permute-done.1
  483.5 8.0 collective-permute-done.1
  493.7 8.0 collective-permute-done.1
  507.6 4.8 multiply_reduce_fusion.10
  515.9 20.0 %multiply_reduce_fusion.1 = (f32[4,12,256]{2,1,0:T(8,128)}, f32[4,12,256]{2,1,0:T(8,128)}, f32[4,12,256]{2,1,0:T(8,128)}, f32[4,256,256]{2,1,0:T(8,128)S(1)}) fusion(f32[4,12,256]{2,1,0:T(8,128)S(1)} %copy-done.59, f32[4,12,256]{2,1,0:T(8,128)S(1)} %copy-done.58, pred[256,256]{1,0:T(8,128)(4,1)S(1)} %copy-done.62, f32[4,256,256]{2,1,0:T(8,128)S(1)} %copy-done.48, ...), kind=kOutput, calls=%fused_computation.9 | convolution fusion | flops 2453368832 | bytes 8699904 | tf_op jit(solution)/shard_map/kihp,kjhp->khij/dot_general | solution.py:168
  540.5 12.9 %fusion.49 = f32[4,256,12,64]{1,3,2,0:T(8,128)} fusion(f32[4,256,12,64]{1,3,2,0:T(8,128)S(1)} %get-tuple-element.158, f32[4,256,12,64]{1,0,3,2:T(4,128)S(1)} %copy-done.9, f32[4,12,256]{2,1,0:T(8,128)S(1)} %copy-done.60, f32[4,12,256]{2,1,0:T(8,128)S(1)} %copy-done.58, f32[4,256,256]{2,1,0:T(8,128)S(1)} %copy-done.48, pred[256,256]{1,0:T(8,128)(4,1)S(1)} %copy-done.62, ...), kind=kOutput, calls=%fused_computation.78 | convolution fusion | flops 2434793472 | bytes 10698800 | tf_op jit(solution)/shard_map/khij,kihp->kjhp/dot_general | solution.py:169
  567.5 4.2 multiply_reduce_fusion.13
  578.1 3.7 copy.290
  586.2 35.3 %all-reduce.9.cloned.1.call-done = f32[1024,256]{1,0:T(8,128)} async-done(((f32[1024,256]{1,0:T(8,128)}), f32[1024,256]{1,0:T(8,128)}) %all-reduce.9.cloned.1.call-update) | async-done | bytes 1048592 | tf_op jit(solution)/shard_map/psum | solution.py:217
  621.6 10.5 multiply_reduce_fusion.3
  637.6 7.6 fusion.37
  647.7 7.5 fusion.69
  655.3 15.0 %copy.307 = f32[1536,2,768]{2,1,0:T(2,128)} copy(f32[1536,2,768]{0,2,1:T(8,128)} %bitcast.208) | data formatting | bytes 18874368 | tf_op jit(solution)/shard_map/reshape | solution.py:250
  670.3 7.9 fusion.70
  678.3 4.0 convolution_add_fusion.1
  682.9 7.9 fusion.83
  693.0 4.1 fusion.102
  698.9 114.5 %all-reduce.13.cloned.1.call-done = f32[1536,2,768]{2,1,0:T(2,128)} async-done(((f32[1536,2,768]{2,1,0:T(2,128)}), f32[1536,2,768]{2,1,0:T(2,128)}) %all-reduce.13.cloned.1.call-update) | async-done | bytes 9437200
  816.1 222.5 %all-reduce.11.cloned.1.call-done = f32[1024,1536]{1,0:T(8,128)} async-done(((f32[1024,1536]{1,0:T(8,128)}), f32[1024,1536]{1,0:T(8,128)}) %all-reduce.11.cloned.1.call-update) | async-done | bytes 6291472 | tf_op jit(solution)/shard_map/psum | solution.py:243
  1038.6 6.5 fusion.14
  1045.1 25.4 %all-reduce.1 = (f32[1536]{0:T(1024)}, f32[5,768]{1,0:T(8,128)}, f32[5,256]{1,0:T(8,128)}, f32[12]{0:T(128)}, f32[12]{0:T(128)}, /*index=5*/f32[12]{0:T(128)}, f32[768]{0:T(1024)}) all-reduce(f32[1536]{0:T(1024)S(1)} %get-tuple-element.75, f32[5,768]{1,0:T(8,128)S(1)} %slice.249, ...), channel_id=1, replica_groups=mesh['dp'=8,'tensor'=4] {'dp'}, use_global_device_ids=true, to_apply=%region_25.26 | all-reduce | flops 7460 | bytes 59680 | tf_op jit(solution)/shard_map/psum | solution.py:267
  1070.5 7.0 fusion.19
  1077.5 17.7 %reduce-scatter.8.cloned.1.call-done = f32[192,768]{1,0:T(8,128)} async-done(((f32[1536,768]{1,0:T(8,128)}), f32[192,768]{1,0:T(8,128)}) %reduce-scatter.8.cloned.1.call-update) | async-done | bytes 589840 | tf_op jit(solution)/shard_map/reduce_scatter | solution.py:257
  1095.2 42.2 %reduce-scatter.6.cloned.1.call-done = f32[192,256]{1,0:T(8,128)} async-done(((f32[1536,256]{1,0:T(8,128)}), f32[192,256]{1,0:T(8,128)}) %reduce-scatter.6.cloned.1.call-update) | async-done | bytes 196624 | tf_op jit(solution)/shard_map/reduce_scatter | solution.py:255
  (374 shorter events, 150.2 us)
Async XLA Ops:
  7.2 156.0 %copy-start = (bf16[1536,768]{1,0:T(8,128)(2,1)S(1)}, bf16[1536,768]{1,0:T(8,128)(2,1)}, u32[]{:S(2)}) copy-start(bf16[1536,768]{1,0:T(8,128)(2,1)} %param.30) | copy-start | bytes 7077892
  7.2 397.0 %all-reduce.7.cloned.1.call-start = ((), (), s32[]{:S(2)}) async-start(), calls=%async_computation.3 | async-start | bytes 12582912 | tf_op jit(solution)/shard_map/psum | solution.py:146
  24.5 19.6 %collective-permute-start.2 = (bf16[3,1024]{1,0:T(4,128)(2,1)S(1)}, bf16[3,1024]{1,0:T(4,128)(2,1)}, u32[]{:S(2)}, u32[]{:S(2)}) collective-permute-start(bf16[3,1024]{1,0:T(4,128)(2,1)S(1)} %pad_maximum_fusion.5), channel_id=1, source_target_pairs={{0,4},{4,8},{8,12},{12,16},{16,20},{20,24},{24,28},{1,5},{5,9},{9,... | collective-permute-start | bytes 18440 | tf_op jit(solution)/shard_map/ppermute | solution.py:18
  34.3 12.0 %copy-start.35 = (f32[4,12,256]{1,0,2:T(4,128)}, f32[4,12,256]{1,0,2:T(4,128)S(1)}, u32[]{:S(2)}) copy-start(f32[4,12,256]{1,0,2:T(4,128)S(1)} %copy.271) | copy-start | bytes 147460
  35.7 10.6 copy-start.65
  35.7 10.6 copy-start.67
  37.4 32.0 %copy-start.72 = (f32[12]{0:T(128)}, f32[12]{0:T(128)S(1)}, u32[]{:S(2)}) copy-start(f32[12]{0:T(128)S(1)} %get-tuple-element.152) | copy-start | bytes 148
  41.5 21.6 %copy-start.51 = (f32[4,256,12]{1,2,0:T(8,128)}, f32[4,256,12]{1,2,0:T(8,128)S(1)}, u32[]{:S(2)}) copy-start(f32[4,256,12]{1,2,0:T(8,128)S(1)} %copy.274) | copy-start | bytes 147460
  52.5 10.6 copy-start.15
  69.8 6.0 collective-permute-start
  75.8 6.6 collective-permute-start
  82.6 9.1 collective-permute-start
  91.8 9.1 collective-permute-start
  101.0 9.1 collective-permute-start
  110.2 9.1 collective-permute-start
  119.4 9.1 collective-permute-start
  131.2 18.7 %copy-start.47 = (f32[4,256,256]{2,1,0:T(8,128)}, f32[4,256,256]{2,1,0:T(8,128)S(1)}, u32[]{:S(2)}) copy-start(f32[4,256,256]{2,1,0:T(8,128)S(1)} %fusion.141) | copy-start | bytes 3145732
  134.9 15.1 %copy-start.21 = (f32[4,256,12,64]{1,3,2,0:T(8,128)}, f32[4,256,12,64]{1,3,2,0:T(8,128)S(1)}, u32[]{:S(2)}) copy-start(f32[4,256,12,64]{1,3,2,0:T(8,128)S(1)} %fusion.134) | copy-start | bytes 9437188
  167.8 453.7 %all-reduce.9.cloned.1.call-start = ((), (), s32[]{:S(2)}) async-start(), calls=%async_computation.4 | async-start | bytes 2097152 | tf_op jit(solution)/shard_map/psum | solution.py:217
  180.6 230.7 %copy-start.75 = (f32[1024]{0:T(1024)}, f32[1024]{0:T(1024)S(1)}, u32[]{:S(2)}) copy-start(f32[1024]{0:T(1024)S(1)} %add_rsqrt_fusion) | copy-start | bytes 12292
  404.2 8.9 copy-start.20
  404.2 9.7 copy-start.39
  437.6 3.8 collective-permute-start.1
  442.3 8.6 collective-permute-start.1
  451.8 9.3 collective-permute-start.1
  461.9 9.3 collective-permute-start.1
  472.1 9.3 collective-permute-start.1
  482.2 9.3 collective-permute-start.1
  492.4 9.3 collective-permute-start.1
  515.9 20.1 %copy-start.24 = (f32[1,12,64,128]{3,2,1,0:T(8,128)S(1)}, f32[1,12,64,128]{3,2,1,0:T(8,128)}, u32[]{:S(2)}) copy-start(f32[1,12,64,128]{3,2,1,0:T(8,128)} %get-tuple-element.120) | copy-start | bytes 1179652
  515.9 20.1 %copy-start.27 = (f32[1,12,64,128]{3,2,1,0:T(8,128)S(1)}, f32[1,12,64,128]{3,2,1,0:T(8,128)}, u32[]{:S(2)}) copy-start(f32[1,12,64,128]{3,2,1,0:T(8,128)} %get-tuple-element.121) | copy-start | bytes 1179652
  515.9 20.1 %copy-start.30 = (f32[1,12,64,128]{3,2,1,0:T(8,128)S(1)}, f32[1,12,64,128]{3,2,1,0:T(8,128)}, u32[]{:S(2)}) copy-start(f32[1,12,64,128]{3,2,1,0:T(8,128)} %get-tuple-element.122) | copy-start | bytes 1179652
  515.9 20.1 %copy-start.33 = (f32[1,12,64,128]{3,2,1,0:T(8,128)S(1)}, f32[1,12,64,128]{3,2,1,0:T(8,128)}, u32[]{:S(2)}) copy-start(f32[1,12,64,128]{3,2,1,0:T(8,128)} %copy-done.32) | copy-start | bytes 1179652
  559.6 137.6 %reduce-scatter.10.cloned.1.call-start = ((), (), s32[]{:S(2)}) async-start(), calls=%async_computation.8 | async-start | bytes 884736
  561.9 9.9 copy-start.25
  561.9 9.9 copy-start.28
  621.6 13.7 %copy-start.7 = (bf16[1024,1536]{1,0:T(8,128)(2,1)S(1)}, bf16[1024,1536]{1,0:T(8,128)(2,1)}, u32[]{:S(2)}) copy-start(bf16[1024,1536]{1,0:T(8,128)(2,1)} %copy-done.6) | copy-start | bytes 9437188
  634.0 3.6 collective-permute-start.3
  637.3 176.1 %all-reduce.13.cloned.1.call-start = ((), (), s32[]{:S(2)}) async-start(), calls=%async_computation.9 | async-start | bytes 18874368
  645.4 9.9 copy-start.45
  670.3 368.3 %all-reduce.11.cloned.1.call-start = ((), (), s32[]{:S(2)}) async-start(), calls=%async_computation.5 | async-start | bytes 12582912 | tf_op jit(solution)/shard_map/psum | solution.py:243
  682.3 412.9 %reduce-scatter.8.cloned.1.call-start = ((), (), s32[]{:S(2)}) async-start(), calls=%async_computation.7 | async-start | bytes 5308416 | tf_op jit(solution)/shard_map/reduce_scatter | solution.py:257
  690.9 446.5 %reduce-scatter.6.cloned.1.call-start = ((), (), s32[]{:S(2)}) async-start(), calls=%async_computation.6 | async-start | bytes 1769472 | tf_op jit(solution)/shard_map/reduce_scatter | solution.py:255
  697.1 341.5 %copy-start.50 = (bf16[1536,256]{1,0:T(8,128)(2,1)S(1)}, bf16[1536,256]{1,0:T(8,128)(2,1)}, u32[]{:S(2)}) copy-start(bf16[1536,256]{1,0:T(8,128)(2,1)} %param.22) | copy-start | bytes 2359300
  697.1 341.5 %copy-start.57 = (f32[1536]{0:T(1024)S(1)}, f32[1536]{0:T(1024)}, u32[]{:S(2)}) copy-start(f32[1536]{0:T(1024)} %param.20) | copy-start | bytes 18436
  697.1 341.5 %copy-start.64 = (f32[1024]{0:T(1024)S(1)}, f32[1024]{0:T(1024)}, u32[]{:S(2)}) copy-start(f32[1024]{0:T(1024)} %copy-done.63) | copy-start | bytes 12292
  816.1 229.0 %copy-start.88 = (f32[768]{0:T(1024)S(1)}, f32[768]{0:T(1024)}, u32[]{:S(2)}) copy-start(f32[768]{0:T(1024)} %get-tuple-element.126) | copy-start | bytes 9220
  1070.5 66.9 %copy-start.1 = (bf16[1536,768]{1,0:T(8,128)(2,1)S(1)}, bf16[1536,768]{1,0:T(8,128)(2,1)}, u32[]{:S(2)}) copy-start(bf16[1536,768]{1,0:T(8,128)(2,1)} %param.30) | copy-start | bytes 7077892
  (80 other events, 295.5 us)
Sparse Core Ops, SparseCore 0:
  168.0 236.1 all-reduce.6
  559.7 61.8 all-reduce.8
  637.4 34.9 reduce-scatter.9
  675.7 137.6 all-reduce.12
  815.6 222.9 all-reduce.10
  1042.4 52.7 reduce-scatter.7
  1099.1 38.3 reduce-scatter.5
where the time goes:
time: 1150 us; the launch traced here: 1140 us
  waiting for transfers between devices  715 us (62%)
  matrix products  139 us (12%)
  local copies, waits for them, and re-layouts  97 us (8%)
  other arithmetic  75.5 us (7%)
  starting transfers between devices  63.3 us (6%)
  blocking collectives  37.4 us (3%)
  between operations  16.7 us (1%)
    psum x1, waiting for transfers between devices, shards(): lax.psum((partial_proj, jnp.sum(gated_out * gated_out, axis=1)), 'tensor')  224 us
    psum x1, waiting for transfers between devices, shards(): lax.psum(grad_normed_part, 'tensor') + product_nt(grad_bc_low, bc_proj)  222 us
    unnamed x9, waiting for transfers between devices  115 us
    ppermute x16, starting transfers between devices, shifted(): return lax.ppermute(x, axis, pairs)  62.3 us
    ppermute x16, waiting for transfers between devices, shifted(): return lax.ppermute(x, axis, pairs)  59 us
    reduce_scatter x1, waiting for transfers between devices, shards(): lax.psum_scatter(grad_bc_local, 'dp', scatter_dimension=0, tiled=True)  42.2 us
    psum x1, waiting for transfers between devices, shards(): lax.psum(jnp.concatenate([grad_b, grad_c], axis=2).reshape(tokens, 2 * st...  35.3 us
    unnamed x222, local copies, waits for them, and re-layouts  32 us
  transfers between devices with their start and end apart: 23, of which 20 were waited for; matrix products, arithmetic and copies ran while one was open for 10% of the time, Pallas kernels for 0%

commit v1 on v0

--- a/solution.py
+++ b/solution.py
@@ -16,6 +16,58 @@
     length = lax.axis_size(axis)
     pairs = [(i, i + by) for i in range(length) if 0 <= i + by < length]
     return lax.ppermute(x, axis, pairs)
+
+
+def exchange(x, axis, bit):
+    length = lax.axis_size(axis)
+    return lax.ppermute(x, axis, [(i, i ^ bit) for i in range(length)])
+
+
+def entering(own, decay, axis, reverse):
+    position = lax.axis_index(axis) % SEQ_DEVS
+    shape = own.shape
+    wide = (decay.shape[0],) + (1,) * (len(shape) - 1)
+    before = jnp.zeros_like(own)
+    before_decay = jnp.ones_like(decay)
+    total = own
+    total_decay = decay
+    bit = 1
+    while bit < SEQ_DEVS:
+        other = exchange(total, axis, bit)
+        other_decay = exchange(total_decay, axis, bit)
+        later = (position & bit) != 0
+        if reverse:
+            later = jnp.logical_not(later)
+        before = jnp.where(later, before + before_decay.reshape(wide) * other, before)
+        before_decay = jnp.where(later, before_decay * other_decay, before_decay)
+        total = jnp.where(
+            later,
+            total + total_decay.reshape(wide) * other,
+            other + other_decay.reshape(wide) * total,
+        )
+        total_decay = total_decay * other_decay
+        bit = bit * 2
+    return before
+
+
+def fold(pieces, axis, bit, mine):
+    sent = lax.dynamic_index_in_dim(pieces, 1 - mine, 0, keepdims=False)
+    kept = lax.dynamic_index_in_dim(pieces, mine, 0, keepdims=False)
+    return kept + exchange(sent.astype(jnp.bfloat16), axis, bit).astype(jnp.float32)
+
+
+def halving_sum(local, axis):
+    length = lax.axis_size(axis)
+    index = lax.axis_index(axis)
+    rows, width = local.shape
+    kept = local.reshape(length, rows // length, width)
+    bit = 1
+    while bit < length:
+        count = kept.shape[0] // 2
+        pieces = jnp.swapaxes(kept.reshape((count, 2) + kept.shape[1:]), 0, 1)
+        kept = fold(pieces, axis, bit, (index // bit) % 2)
+        bit = bit * 2
+    return kept[0]
 
 
 def swish_value(operand):
@@ -122,13 +174,7 @@
         decay_before.append(decay_before[-1] * block_decay[block_index])
     own_state = local_in[blocks]
     own_decay = decay_before[blocks]
-    entry_decay = jnp.where(opens_seq, 0.0, own_decay)
-
-    def relay_state(turn_index, incoming):
-        return shifted(entry_decay[:, None, None] * incoming + own_state, "dp", 1)
-
-    arrived = lax.fori_loop(0, SEQ_DEVS - 1, relay_state, jnp.zeros_like(own_state))
-    arrived = jnp.where(opens_seq, 0.0, arrived)
+    arrived = entering(own_state, own_decay, "dp", False)
     states_in = (
         jnp.stack(local_in[:blocks]) + jnp.stack(decay_before[:blocks])[:, :, None, None] * arrived
     )
@@ -142,15 +188,30 @@
     gate_act = swish_value(gate_wide)
     gated_out = ssd_flat * gate_act
     gated_low = (gated_out * gate_gain).astype(jnp.bfloat16)
+    grad_top = cotangent.astype(jnp.float32)
     partial_proj = product_nt(gated_low, out_proj)
-    proj_sum, square_sum = lax.psum(
-        (partial_proj, jnp.sum(gated_out * gated_out, axis=1)), "tensor"
+    square_sum, grad_inv = lax.psum(
+        (jnp.sum(gated_out * gated_out, axis=1), jnp.sum(grad_top * partial_proj, axis=1)),
+        "tensor",
     )
     inv_gate = lax.rsqrt(square_sum / inner_total + EPSILON)[:, None]
-    block_out = (residual + inv_gate * proj_sum).astype(jnp.bfloat16)
-    grad_top = cotangent.astype(jnp.float32)
+    parts = lax.axis_size("tensor")
+    own_rows = tokens // parts
+    first_row = lax.axis_index("tensor") * own_rows
+
+    def rows_of(array):
+        return lax.dynamic_slice_in_dim(array, first_row, own_rows, 0)
+
+    def row_sums(partial):
+        return lax.psum_scatter(
+            partial.astype(jnp.bfloat16), "tensor", scatter_dimension=0, tiled=True
+        ).astype(jnp.float32)
+
+    proj_rows = row_sums(partial_proj)
+    out_rows = (rows_of(residual) + rows_of(inv_gate) * proj_rows).astype(jnp.bfloat16)
+    block_out = lax.all_gather(out_rows, "tensor", axis=0, tiled=True)
     grad_proj = (inv_gate * grad_top).astype(jnp.bfloat16)
-    grad_inv = jnp.sum(grad_top * proj_sum, axis=1, keepdims=True)
+    grad_inv = grad_inv[:, None]
     grad_gated_low = jnp.dot(grad_proj, out_proj, preferred_element_type=jnp.float32)
     grad_out_local = product_tn(grad_proj, gated_low)
     grad_gate_gain = jnp.sum(grad_gated_low * gated_out, axis=0)
@@ -186,13 +247,7 @@
         )
         decay_after.insert(0, decay_after[0] * block_decay[block_index])
     own_grad = local_grad[0]
-    exit_decay = jnp.where(closes_seq, 0.0, own_decay)
-
-    def relay_grad(turn_index, incoming):
-        return shifted(exit_decay[:, None, None] * incoming + own_grad, "dp", -1)
-
-    back_arrived = lax.fori_loop(0, SEQ_DEVS - 1, relay_grad, jnp.zeros_like(own_grad))
-    back_arrived = jnp.where(closes_seq, 0.0, back_arrived)
+    back_arrived = entering(own_grad, own_decay, "dp", True)
     grad_states = jnp.stack(local_grad) + jnp.stack(decay_after)[:, :, None, None] * back_arrived
     grad_send = grad_states[1:]
     state_back = jnp.einsum("khpn,kjn->kjhp", grad_send, b_rows, precision=PRECISE)
@@ -240,22 +295,30 @@
     grad_bc_low = grad_conv_in[:, inner_local:].astype(jnp.bfloat16)
     grad_zx_low = jnp.concatenate([grad_gate, grad_inner_low], axis=1)
     grad_normed_part = product_nt(grad_zx_low, zx_flat) + product_nt(grad_dt_low, dt_proj)
-    grad_normed = lax.psum(grad_normed_part, "tensor") + product_nt(grad_bc_low, bc_proj)
-    grad_norm_local = jnp.sum(grad_normed * normed, axis=0)
+    grad_normed_part, block_out = lax.optimization_barrier((grad_normed_part, block_out))
+    grad_normed = row_sums(grad_normed_part) + product_nt(rows_of(grad_bc_low), bc_proj)
+    normed_rows = rows_of(normed)
+    grad_norm_local = jnp.sum(grad_normed * normed_rows, axis=0)
     grad_scaled_in = grad_normed * norm_gain
-    grad_resid = inv_rms * (
-        grad_scaled_in - normed * jnp.mean(grad_scaled_in * normed, axis=1, keepdims=True)
-    )
-    grad_hidden = (grad_top + grad_resid).astype(jnp.bfloat16)
-    grad_zx_local = product_tn(normed_low, grad_zx_low).reshape(model_width, 2, inner_local)
+    grad_resid = rows_of(inv_rms) * (
+        grad_scaled_in - normed_rows * jnp.mean(grad_scaled_in * normed_rows, axis=1, keepdims=True)
+    )
+    hidden_rows = (rows_of(grad_top) + grad_resid).astype(jnp.bfloat16)
+    grad_hidden = lax.all_gather(hidden_rows, "tensor", axis=0, tiled=True)
+    grad_norm_local = lax.psum(grad_norm_local, "tensor")
+    low = jnp.bfloat16
+    grad_z_local = product_tn(normed_low, grad_gate)
+    grad_x_local = product_tn(normed_low, grad_inner_low)
     grad_bc_local = product_tn(normed_low, grad_bc_low)
     grad_dt_local = product_tn(normed_low, grad_dt_low)
-    grad_zx_proj, grad_bc_proj, grad_dt_proj, grad_out_proj = (
-        lax.psum_scatter(grad_zx_local, "dp", scatter_dimension=0, tiled=True),
-        lax.psum_scatter(grad_bc_local, "dp", scatter_dimension=0, tiled=True),
-        lax.psum_scatter(grad_dt_local, "dp", scatter_dimension=0, tiled=True),
-        lax.psum_scatter(grad_out_local, "dp", scatter_dimension=0, tiled=True),
-    )
+
+    def spread_sum(local):
+        return halving_sum(local, "dp")
+
+    grad_out_proj = spread_sum(grad_out_local)
+    grad_zx_proj = jnp.stack([spread_sum(grad_z_local), spread_sum(grad_x_local)], axis=1)
+    grad_bc_proj = spread_sum(grad_bc_local)
+    grad_dt_proj = spread_sum(grad_dt_local)
     (
         grad_norm_gain,
         grad_conv_x,

time: 1150 us -> 538 us (0.47)
  waiting for transfers between devices: 715 us -> 135 us
  starting transfers between devices: 63.3 us -> 24.6 us
  local copies, waits for them, and re-layouts: 97 us -> 79 us
  other arithmetic: 75.5 us -> 90.9 us
    psum x2 -> x0, waiting for transfers between devices: 446 us -> none  [the longest x1 224 us: shards(): lax.psum((partial_proj, jnp.sum(gated_out * gated_out, axis=1)), 'tensor')]
    unnamed x9 -> x5, waiting for transfers between devices: 115 us -> 0.08 us
    ppermute x16 -> x2, starting transfers between devices: 62.3 us -> 4.26 us  [shifted(): return lax.ppermute(x, axis, pairs)]
    ppermute x16 -> x2, waiting for transfers between devices: 59 us -> 1.05 us  [shifted(): return lax.ppermute(x, axis, pairs)]
    reduce_scatter x2, waiting for transfers between devices: 59.9 us -> 15.9 us  [row_sums(): lax.psum_scatter(partial.astype(jnp.bfloat16), 'tensor', scatter_dimensio...]
    ppermute x0 -> x23, waiting for transfers between devices: none -> 43.8 us  [exchange(): return lax.ppermute(x, axis, [(i, i ^ bit) for i in range(length)])]
    all_gather x0 -> x2, waiting for transfers between devices: none -> 37.3 us  [the longest x1 37.3 us: shards(): block_out = lax.all_gather(out_rows, 'tensor', axis=0, tiled=True)]
    ppermute x0 -> x23, starting transfers between devices: none -> 20 us  [exchange(): return lax.ppermute(x, axis, [(i, i ^ bit) for i in range(length)])]
  transfers between devices with their start and end apart: 23 -> 30, of which waited for: 20 -> 14; matrix products, arithmetic and copies ran while one was open for 10% -> 36% of each run, Pallas kernels for 0% -> 0%
where the time goes in v1:
time: 538 us; the launch traced here: 529 us
  matrix products  137 us (25%)
  waiting for transfers between devices  135 us (25%)
  other arithmetic  90.9 us (17%)
  local copies, waits for them, and re-layouts  79 us (15%)
  blocking collectives  47.5 us (9%)
  starting transfers between devices  24.6 us (5%)
  between operations  15.8 us (3%)
    ppermute x23, waiting for transfers between devices, exchange(): return lax.ppermute(x, axis, [(i, i ^ bit) for i in range(length)])  43.8 us
    all_gather x1, waiting for transfers between devices, shards(): block_out = lax.all_gather(out_rows, 'tensor', axis=0, tiled=True)  37.3 us
    psum x1, waiting for transfers between devices, shards(): lax.psum(jnp.concatenate([grad_b, grad_c], axis=2).reshape(tokens, 2 * st...  36.3 us
    unnamed x233, local copies, waits for them, and re-layouts  26.9 us
    psum x1, blocking collectives, shards(): lax.psum((grad_norm_local, grad_taps[:, :inner_local], grad_taps[:, inner...  24.1 us
    dot_general x1, matrix products, shards(): jnp.einsum('kihp,kjhp->khij', grad_ssd, inputs, precision=PRECISE)  23.1 us
    ppermute x23, starting transfers between devices, exchange(): return lax.ppermute(x, axis, [(i, i ^ bit) for i in range(length)])  20 us
    dot_general x4, matrix products, product_nt(): lax.dot_general(first_op, second_op, (((1,), (1,)), ((), ())), preferred_...  16.9 us
  transfers between devices with their start and end apart: 30, of which 14 were waited for; matrix products, arithmetic and copies ran while one was open for 36% of the time, Pallas kernels for 0%

profile of v1, /device:TPU:0, one launch (start us, length us, event | category | flops | bytes accessed | tf_op | source)
XLA Modules:
  0.0 529.2 jit_solution(9152950285722818605)
XLA Ops:
  7.3 3.4 copy.408
  13.5 5.5 %convolution_convert_fusion = bf16[1024,1536]{1,0:T(8,128)(2,1)S(1)} fusion(bf16[1536,1536]{1,0:T(8,128)(2,1)S(1)} %bitcast.307, f32[1536]{0:T(1024)S(1)} %copy-done.62, f32[1024]{0:T(1024)S(1)} %add_rsqrt_fusion.1, bf16[1024,1536]{1,0:T(8,128)(2,1)S(1)} %copy-done.7), kind=kOutput, calls=%fused_computation.49 | convolution fusion | flops 4839702528 | bytes 11020288 | tf_op jit(solution)/shard_map/dot_general | solution.py:125
  19.8 3.0 collective-permute-start
  35.3 4.0 fusion.27
  43.4 3.5 copy.336
  46.9 5.3 reshape.329
  52.2 5.0 fusion.47
  69.0 5.5 %convert_element_type.182 = f32[1024,1536]{1,0:T(8,128)} convert(bf16[1024,1536]{1,0:T(8,128)(2,1)} %param.15) | non-fusion elementwise | flops 1572864 | bytes 9437184 | tf_op jit(solution)/shard_map/convert_element_type | solution.py:120
  77.0 3.0 collective-permute-done.4
  86.1 5.8 %collective-permute-done.5 = f32[12,64,128]{2,1,0:T(8,128)S(1)} collective-permute-done((f32[12,64,128]{2,1,0:T(8,128)S(1)}, f32[12,64,128]{2,1,0:T(8,128)S(1)}, u32[]{:S(2)}, u32[]{:S(2)}) %collective-permute-start.5) | collective-permute-done | bytes 393248 | tf_op jit(solution)/shard_map/ppermute | solution.py:23
  96.8 15.3 %fusion.40 = f32[4,256,12,64]{1,3,2,0:T(8,128)S(1)} fusion(f32[4,256,12,64]{1,3,2,0:T(8,128)S(1)} %fusion.128, f32[4,256,12,64]{1,0,3,2:T(4,128)S(1)} %copy-done.3, f32[4,12,256]{2,1,0:T(8,128)S(1)} %copy-done.56, f32[4,12,256]{2,1,0:T(8,128)S(1)} %copy.341, f32[4,256,256]{2,1,0:T(8,128)S(1)} %fusion.139, pred[256,256]{1,0:T(8,128)(4,1)S(1)} %iota_compare_fusion, ...), kind=kOutput, calls=%fused_computation.64 | convolution fusion | flops 2434793472 | bytes 10698800 | tf_op jit(solution)/shard_map/khij,kjhp->kihp/dot_general | solution.py:162
  116.7 3.6 copy.352
  120.2 3.6 multiply_reduce_fusion.13
  123.9 4.2 fusion.135
  128.1 12.1 %all-reduce.1 = (f32[1024]{0:T(1024)S(1)}, f32[1024]{0:T(1024)S(1)}) all-reduce(f32[1024]{0:T(1024)S(1)} %get-tuple-element.165, f32[1024]{0:T(1024)S(1)} %get-tuple-element.151), channel_id=1, replica_groups=mesh['dp'=8,'tensor'=4] {'tensor'}, use_global_device_ids=true, to_apply=%region_6.7 | all-reduce | flops 2048 | bytes 16384 | tf_op jit(solution)/shard_map/psum | solution.py:193
  140.2 11.0 %multiply_reduce_fusion.10 = (f32[768]{0:T(1024)}, f32[1024,768]{1,0:T(8,128)}, bf16[1024,768]{1,0:T(8,128)(2,1)}, f32[768]{0:T(1024)}) fusion(f32[1024,1024]{1,0:T(8,128)} %copy-done.12, bf16[1024,1536]{1,0:T(8,128)(2,1)} %copy-done.36, f32[1024,768]{1,0:T(8,128)} %copy-done.34, f32[1024]{0:T(1024)S(1)} %get-tuple-element.182, f32[768]{0:T(1024)} %param.25, ...), kind=kOutput, calls=%fused_computation.66 | convolution fusion | flops 2436364800 | bytes 21251072 | tf_op jit(solution)/shard_map/dot_general | solution.py:215
  151.2 3.6 copy.354
  154.8 5.2 reshape.337
  160.0 5.0 fusion.43
  169.0 23.1 %multiply_reduce_fusion.1 = (f32[4,12,256]{2,1,0:T(8,128)S(1)}, f32[4,12,256]{2,1,0:T(8,128)S(1)}, f32[4,12,256]{2,1,0:T(8,128)S(1)}, f32[4,256,256]{2,1,0:T(8,128)}) fusion(f32[4,12,256]{2,1,0:T(8,128)S(1)} %copy-done.57, f32[4,12,256]{2,1,0:T(8,128)S(1)} %copy.341, pred[256,256]{1,0:T(8,128)(4,1)} %copy-done.58, f32[4,256,256]{2,1,0:T(8,128)} %copy-done.48, ...), kind=kOutput, calls=%fused_computation.7 | convolution fusion | flops 2453368832 | bytes 8699904 | tf_op jit(solution)/shard_map/kihp,kjhp->khij/dot_general | solution.py:229
  201.4 5.7 %fusion.76 = f32[4,256,128]{1,2,0:T(8,128)S(1)} fusion(f32[4,256,12,64]{1,0,3,2:T(4,128)} %reshape.337, f32[4,256,12]{1,2,0:T(8,128)S(1)} %copy.346, f32[1,12,64,128]{3,2,1,0:T(8,128)} %copy-done.20, f32[1,12,64,128]{3,2,1,0:T(8,128)} %copy-done.22, f32[1,12,64,128]{3,2,1,0:T(8,128)} %copy-done.24, f32[1,12,64,128]{3,2,1,0:T(8,128)} %copy-done.26, ...), kind=kOutput, calls=%fused_computation.116 | convolution fusion | flops 1210712064 | bytes 5685440 | tf_op jit(solution)/shard_map/kihp,khpn->kin/dot_general | solution.py:226
  212.0 8.1 %collective-permute-done.8 = f32[12,64,128]{2,1,0:T(8,128)S(1)} collective-permute-done((f32[12,64,128]{2,1,0:T(8,128)S(1)}, f32[12,64,128]{2,1,0:T(8,128)S(1)}, u32[]{:S(2)}, u32[]{:S(2)}) %collective-permute-start.8) | collective-permute-done | bytes 393248 | tf_op jit(solution)/shard_map/ppermute | solution.py:23
  221.4 4.8 fusion.73
  228.7 5.9 %multiply_reduce_fusion.12 = (f32[4,256,12]{1,2,0:T(8,128)S(1)}, f32[4,256,12,64]{1,3,2,0:T(8,128)S(1)}) fusion(f32[4,256,12,64]{1,0,3,2:T(4,128)} %reshape.329, f32[4,256,128,1]{2,1,3,0:T(8,128)S(1)} %bitcast.288, f32[5,12,64,128]{3,2,1,0:T(8,128)} %broadcast_dynamic-update-slice_fusion, f32[12,64,128]{2,1,0:T(8,128)S(1)} %add_select_fusion, ...), kind=kOutput, calls=%fused_computation.68 | convolution fusion | flops 1210306560 | bytes 8831168 | tf_op jit(solution)/shard_map/khpn,kjn->kjhp/dot_general | solution.py:253
  234.7 12.4 %fusion.39 = f32[4,256,12,64]{1,3,2,0:T(8,128)S(1)} fusion(f32[4,256,12,64]{1,3,2,0:T(8,128)S(1)} %get-tuple-element.200, f32[4,256,12,64]{1,0,3,2:T(4,128)S(1)} %copy-done.6, f32[4,12,256]{2,1,0:T(8,128)S(1)} %copy-done.57, f32[4,12,256]{2,1,0:T(8,128)S(1)} %copy-done.55, f32[4,256,256]{2,1,0:T(8,128)S(1)} %copy-done.49, ...), kind=kOutput, calls=%fused_computation.62 | convolution fusion | flops 2434793472 | bytes 10698800 | tf_op jit(solution)/shard_map/khij,kihp->kjhp/dot_general | solution.py:230
  251.5 3.6 copy.364
  256.2 3.4 multiply_reduce_fusion.17
  263.0 2.8 add_convert_fusion.1
  269.2 36.3 %all-reduce.4.cloned.1.call-done = f32[1024,256]{1,0:T(8,128)} async-done(((f32[1024,256]{1,0:T(8,128)}), f32[1024,256]{1,0:T(8,128)}) %all-reduce.4.cloned.1.call-update) | async-done | bytes 1048592 | tf_op jit(solution)/shard_map/psum | solution.py:272
  305.6 11.1 %multiply_reduce_fusion.5 = (f32[1024]{0:T(1024)S(1)}, f32[1024]{0:T(1024)}, f32[1024]{0:T(1024)}, f32[1024]{0:T(1024)}, f32[1024]{0:T(1024)}, /*index=5*/f32[1024,1024]{1,0:T(8,128)S(1)}) fusion(f32[1027,1024]{1,0:T(8,128)} %copy-done.2, f32[1024,1024]{1,0:T(8,128)} %get-tuple-element.161, f32[1024,256]{1,0:T(8,128)} %all-reduce.4.cloned.1.call-done, ...), kind=kLoop, calls=%fused_computation.42 | loop fusion | flops 18869248 | bytes 29380608 | tf_op jit(solution)/shard_map/reduce_sum | solution.py:289
  323.5 7.0 %fusion.35 = f32[1024,1536]{1,0:T(8,128)S(1)} fusion(bf16[1536,1536]{1,0:T(8,128)(2,1)} %bitcast.308, bf16[1024,768]{1,0:T(8,128)(2,1)S(1)} %slice.244, bf16[1024,768]{1,0:T(8,128)(2,1)S(1)} %copy-done.108), kind=kOutput, calls=%fused_computation.57 | convolution fusion | flops 4838129664 | bytes 14155776 | tf_op jit(solution)/shard_map/dot_general | solution.py:83
  333.1 37.3 %all-gather.3.cloned.1.call-done = bf16[1024,1536]{1,0:T(8,128)(2,1)} async-done(((bf16[256,1536]{1,0:T(8,128)(2,1)}), bf16[1024,1536]{1,0:T(8,128)(2,1)}) %all-gather.3.cloned.1.call-update) | async-done | bytes 3145744 | tf_op jit(solution)/shard_map/all_gather | solution.py:212
  370.8 5.5 %fusion.131 = f32[1536,768]{1,0:T(8,128)S(1)} fusion(bf16[1024,768]{1,0:T(8,128)(2,1)} %get-tuple-element.162, f32[1536]{0:T(1024)S(1)} %copy-done.62, f32[1024]{0:T(1024)S(1)} %copy-done.68, bf16[1024,1536]{1,0:T(8,128)(2,1)} %param.15), kind=kOutput, calls=%fused_computation.266 | convolution fusion | flops 2422210560 | bytes 9447424 | tf_op jit(solution)/shard_map/dot_general | solution.py:89
  378.9 3.1 fusion.71
  382.6 3.4 broadcast_multiply_fusion
  386.1 3.5 convert_element_type.187
  398.5 3.7 bitcast_add_fusion.2
  403.0 8.3 %collective-permute-done.20 = bf16[2,192,12]{1,0,2:T(2,128)(2,1)S(1)} collective-permute-done((bf16[2,192,12]{1,0,2:T(2,128)(2,1)S(1)}, bf16[2,192,12]{1,0,2:T(2,128)(2,1)S(1)}, u32[]{:S(2)}, u32[]{:S(2)}) %collective-permute-start.20) | collective-permute-done | bytes 9248 | tf_op jit(solution)/shard_map/ppermute | solution.py:23
  416.4 15.8 %reduce-scatter.5.cloned.1.call-done = bf16[256,1536]{1,0:T(8,128)(2,1)} async-done(((bf16[1024,1536]{1,0:T(8,128)(2,1)}), bf16[256,1536]{1,0:T(8,128)(2,1)}) %reduce-scatter.5.cloned.1.call-update) | async-done | bytes 786448 | tf_op jit(solution)/shard_map/reduce_scatter | solution.py:206
  432.3 3.1 multiply_reduce_fusion.14
  435.4 3.2 add_convert_fusion
  440.2 5.3 fusion.129
  453.8 3.9 collective-permute-done.12
  461.4 8.9 %collective-permute-done.14 = bf16[2,192,768]{2,1,0:T(8,128)(2,1)S(1)} collective-permute-done((bf16[2,192,768]{2,1,0:T(8,128)(2,1)S(1)}, bf16[2,192,768]{2,1,0:T(8,128)(2,1)S(1)}, u32[]{:S(2)}, u32[]{:S(2)}) %collective-permute-start.14) | collective-permute-done | bytes 589856 | tf_op jit(solution)/shard_map/ppermute | solution.py:23
  475.3 2.9 collective-permute-done.15
  481.4 11.3 %psum.80 = f32[1536]{0:T(1024)S(1)} all-reduce(f32[1536]{0:T(1024)S(1)} %copy-done.63), channel_id=1, replica_groups=mesh['dp'=8,'tensor'=4] {'tensor'}, use_global_device_ids=true, to_apply=%region_22.23 | all-reduce | flops 1536 | bytes 12288 | tf_op jit(solution)/shard_map/psum | solution.py:308
  492.7 24.1 %all-reduce = (f32[1536]{0:T(1024)}, f32[5,768]{1,0:T(8,128)}, f32[5,256]{1,0:T(8,128)}, f32[12]{0:T(128)}, f32[12]{0:T(128)}, /*index=5*/f32[12]{0:T(128)}, f32[768]{0:T(1024)}) all-reduce(f32[1536]{0:T(1024)S(1)} %psum.80, f32[5,768]{1,0:T(8,128)S(1)} %slice.249, ...), channel_id=1, replica_groups=mesh['dp'=8,'tensor'=4] {'dp'}, use_global_device_ids=true, to_apply=%region_23.24 | all-reduce | flops 7460 | bytes 59680 | tf_op jit(solution)/shard_map/psum | solution.py:330
  516.9 3.9 copy.472
  (424 shorter events, 134.3 us)
Async XLA Ops:
  7.2 116.7 %copy-start = (bf16[1536,768]{1,0:T(8,128)(2,1)S(1)}, bf16[1536,768]{1,0:T(8,128)(2,1)}, u32[]{:S(2)}) copy-start(bf16[1536,768]{1,0:T(8,128)(2,1)} %param.26) | copy-start | bytes 7077892
  7.2 255.8 %reduce-scatter.3.cloned.1.call-start = ((), (), s32[]{:S(2)}) async-start(), calls=%async_computation.3 | async-start | bytes 3932160 | tf_op jit(solution)/shard_map/reduce_scatter | solution.py:206
  19.8 13.2 %collective-permute-start = (bf16[3,1024]{1,0:T(4,128)(2,1)}, bf16[3,1024]{1,0:T(4,128)(2,1)}, u32[]{:S(2)}, u32[]{:S(2)}) collective-permute-start(bf16[3,1024]{1,0:T(4,128)(2,1)} %pad_maximum_fusion.3), channel_id=1, source_target_pairs={{0,4},{4,8},{8,12},{12,16},{16,20},{20,24},{24,28},{1,5},{5,9},{9,... | collective-permute-start | bytes 18440 | tf_op jit(solution)/shard_map/ppermute | solution.py:18
  30.1 33.7 %copy-start.64 = (f32[12]{0:T(128)}, f32[12]{0:T(128)S(1)}, u32[]{:S(2)}) copy-start(f32[12]{0:T(128)S(1)} %get-tuple-element.190) | copy-start | bytes 148
  59.4 4.3 collective-permute-start.1
  62.2 1.6 collective-permute-start.2
  66.9 13.7 %collective-permute-start.3 = (f32[12,64,128]{2,1,0:T(8,128)}, f32[12,64,128]{2,1,0:T(8,128)S(1)}, u32[]{:S(2)}, u32[]{:S(2)}) collective-permute-start(f32[12,64,128]{2,1,0:T(8,128)} %add_select_fusion.7), channel_id=1, source_target_pairs={{0,8},{4,12},{8,0},{12,4},{16,24},{20,28},{24,16},{28,20},{1,9},{5... | collective-permute-start | bytes 1179656 | tf_op jit(solution)/shard_map/ppermute | solution.py:23
  68.9 100.0 %copy-start.54 = (f32[4,12,256]{2,1,0:T(8,128)}, f32[4,12,256]{2,1,0:T(8,128)S(1)}, u32[]{:S(2)}) copy-start(f32[4,12,256]{2,1,0:T(8,128)S(1)} %copy.341) | copy-start | bytes 147460
  76.4 15.6 %copy-start.46 = (f32[12,64,128]{2,1,0:T(8,128)S(1)}, f32[12,64,128]{2,1,0:T(8,128)}, u32[]{:S(2)}) copy-start(f32[12,64,128]{2,1,0:T(8,128)} %copy-done.45) | copy-start | bytes 1179652
  76.4 20.3 %copy-start.58 = (pred[256,256]{1,0:T(8,128)(4,1)}, pred[256,256]{1,0:T(8,128)(4,1)S(1)}, u32[]{:S(2)}) copy-start(pred[256,256]{1,0:T(8,128)(4,1)S(1)} %iota_compare_fusion) | copy-start | bytes 196612
  76.4 3.6 collective-permute-start.4
  81.9 10.0 %collective-permute-start.5 = (f32[12,64,128]{2,1,0:T(8,128)S(1)}, f32[12,64,128]{2,1,0:T(8,128)S(1)}, u32[]{:S(2)}, u32[]{:S(2)}) collective-permute-start(f32[12,64,128]{2,1,0:T(8,128)S(1)} %add_select_fusion.6), channel_id=1, source_target_pairs={{0,16},{4,20},{8,24},{12,28},{16,0},{20,4},{24,8},{28,12},{1,17},{... | collective-permute-start | bytes 1179656 | tf_op jit(solution)/shard_map/ppermute | solution.py:23
  96.7 15.3 %copy-start.16 = (f32[4,256,12,64]{1,3,2,0:T(8,128)}, f32[4,256,12,64]{1,3,2,0:T(8,128)S(1)}, u32[]{:S(2)}) copy-start(f32[4,256,12,64]{1,3,2,0:T(8,128)S(1)} %fusion.128) | copy-start | bytes 9437188
  167.0 26.9 %collective-permute-start.6 = (f32[12,64,128]{2,1,0:T(8,128)}, f32[12,64,128]{2,1,0:T(8,128)}, u32[]{:S(2)}, u32[]{:S(2)}) collective-permute-start(f32[12,64,128]{2,1,0:T(8,128)} %fusion.102), channel_id=1, source_target_pairs={{0,4},{4,0},{8,12},{12,8},{16,20},{20,16},{24,28},{28,24},{1,5},{5... | collective-permute-start | bytes 1179656 | tf_op jit(solution)/shard_map/ppermute | solution.py:23
  167.1 138.5 %all-reduce.4.cloned.1.call-start = ((), (), s32[]{:S(2)}) async-start(), calls=%async_computation.2 | async-start | bytes 2097152 | tf_op jit(solution)/shard_map/psum | solution.py:272
  169.0 23.1 %copy-start.33 = (f32[1,12,64,128]{3,2,1,0:T(8,128)S(1)}, f32[1,12,64,128]{3,2,1,0:T(8,128)}, u32[]{:S(2)}) copy-start(f32[1,12,64,128]{3,2,1,0:T(8,128)} %get-tuple-element.150) | copy-start | bytes 1179652
  169.0 23.8 %copy-start.5 = (f32[4,256,12,64]{1,0,3,2:T(4,128)S(1)}, f32[4,256,12,64]{1,0,3,2:T(4,128)}, u32[]{:S(2)}) copy-start(f32[4,256,12,64]{1,0,3,2:T(4,128)} %reshape.337) | copy-start | bytes 9437188
  169.0 23.8 %copy-start.17 = (f32[4,256,12,64]{1,3,2,0:T(8,128)S(1)}, f32[4,256,12,64]{1,3,2,0:T(8,128)}, u32[]{:S(2)}) copy-start(f32[4,256,12,64]{1,3,2,0:T(8,128)} %copy-done.16) | copy-start | bytes 9437188
  195.9 11.9 %collective-permute-start.7 = (f32[12,64,128]{2,1,0:T(8,128)}, f32[12,64,128]{2,1,0:T(8,128)}, u32[]{:S(2)}, u32[]{:S(2)}) collective-permute-start(f32[12,64,128]{2,1,0:T(8,128)} %add_select_fusion.5), channel_id=1, source_target_pairs={{0,8},{4,12},{8,0},{12,4},{16,24},{20,28},{24,16},{28,20},{1,9},{5... | collective-permute-start | bytes 1179656 | tf_op jit(solution)/shard_map/ppermute | solution.py:23
  207.1 14.2 %copy-start.4 = (f32[4,256,12,64]{1,0,3,2:T(4,128)S(1)}, f32[4,256,12,64]{1,0,3,2:T(4,128)}, u32[]{:S(2)}) copy-start(f32[4,256,12,64]{1,0,3,2:T(4,128)} %reshape.329) | copy-start | bytes 9437188
  209.3 10.7 %collective-permute-start.8 = (f32[12,64,128]{2,1,0:T(8,128)S(1)}, f32[12,64,128]{2,1,0:T(8,128)S(1)}, u32[]{:S(2)}, u32[]{:S(2)}) collective-permute-start(f32[12,64,128]{2,1,0:T(8,128)S(1)} %add_select_fusion.4), channel_id=1, source_target_pairs={{0,16},{4,20},{8,24},{12,28},{16,0},{20,4},{24,8},{28,12},{1,17},{... | collective-permute-start | bytes 1179656 | tf_op jit(solution)/shard_map/ppermute | solution.py:23
  256.2 114.3 %all-gather.3.cloned.1.call-start = ((), (), s32[]{:S(2)}) async-start(), calls=%async_computation.4 | async-start | bytes 3932160 | tf_op jit(solution)/shard_map/all_gather | solution.py:212
  265.8 166.4 %reduce-scatter.5.cloned.1.call-start = ((), (), s32[]{:S(2)}) async-start(), calls=%async_computation.5 | async-start | bytes 3932160 | tf_op jit(solution)/shard_map/reduce_scatter | solution.py:206
  316.7 3.1 collective-permute-start.9
  333.1 37.6 %copy-start.68 = (f32[1024]{0:T(1024)S(1)}, f32[1024]{0:T(1024)}, u32[]{:S(2)}) copy-start(f32[1024]{0:T(1024)} %copy-done.67) | copy-start | bytes 12292
  370.5 146.4 %all-gather.5.cloned.1.call-start = ((), (), s32[]{:S(2)}) async-start(), calls=%async_computation.6 | async-start | bytes 3932160 | tf_op jit(solution)/shard_map/all_gather | solution.py:307
  378.8 11.5 %collective-permute-start.10 = (bf16[4,192,768]{2,1,0:T(8,128)(2,1)}, bf16[4,192,768]{2,1,0:T(8,128)(2,1)}, u32[]{:S(2)}, u32[]{:S(2)}) collective-permute-start(bf16[4,192,768]{2,1,0:T(8,128)(2,1)} %fusion.80), channel_id=1, source_target_pairs={{0,4},{4,0},{8,12},{12,8},{16,20},{20,16},{24,28},{28,24},{1,5},{5... | collective-permute-start | bytes 3538952 | tf_op jit(solution)/shard_map/ppermute | solution.py:23
  382.1 16.4 %collective-permute-start.22 = (bf16[4,192,768]{2,1,0:T(8,128)(2,1)S(1)}, bf16[4,192,768]{2,1,0:T(8,128)(2,1)}, u32[]{:S(2)}, u32[]{:S(2)}) collective-permute-start(bf16[4,192,768]{2,1,0:T(8,128)(2,1)S(1)} %fusion.81), channel_id=1, source_target_pairs={{0,4},{4,0},{8,12},{12,8},{16,20},{20,16},{24,28},{28,24},{1,5},{5... | collective-permute-start | bytes 3538952 | tf_op jit(solution)/shard_map/ppermute | solution.py:23
  395.0 43.5 %collective-permute-start.11 = (bf16[2,192,768]{2,1,0:T(8,128)(2,1)}, bf16[2,192,768]{2,1,0:T(8,128)(2,1)}, u32[]{:S(2)}, u32[]{:S(2)}) collective-permute-start(bf16[2,192,768]{2,1,0:T(8,128)(2,1)} %fusion.90), channel_id=1, source_target_pairs={{0,8},{4,12},{8,0},{12,4},{16,24},{20,28},{24,16},{28,20},{1,9},{5... | collective-permute-start | bytes 1769480 | tf_op jit(solution)/shard_map/ppermute | solution.py:23
  397.6 4.6 collective-permute-start.19
  402.3 8.9 %collective-permute-start.20 = (bf16[2,192,12]{1,0,2:T(2,128)(2,1)S(1)}, bf16[2,192,12]{1,0,2:T(2,128)(2,1)S(1)}, u32[]{:S(2)}, u32[]{:S(2)}) collective-permute-start(bf16[2,192,12]{1,0,2:T(2,128)(2,1)S(1)} %bitcast.346), channel_id=1, source_target_pairs={{0,8},{4,12},{8,0},{12,4},{16,24},{20,28},{24,16},{28,20},{1,9},{5... | collective-permute-start | bytes 27656 | tf_op jit(solution)/shard_map/ppermute | solution.py:23
  411.3 4.4 collective-permute-start.21
  414.2 35.1 %collective-permute-start.23 = (bf16[2,192,768]{2,1,0:T(8,128)(2,1)S(1)}, bf16[2,192,768]{2,1,0:T(8,128)(2,1)}, u32[]{:S(2)}, u32[]{:S(2)}) collective-permute-start(bf16[2,192,768]{2,1,0:T(8,128)(2,1)S(1)} %fusion.91), channel_id=1, source_target_pairs={{0,8},{4,12},{8,0},{12,4},{16,24},{20,28},{24,16},{28,20},{1,9},{5... | collective-permute-start | bytes 1769480 | tf_op jit(solution)/shard_map/ppermute | solution.py:23
  445.6 7.3 %collective-permute-start.13 = (bf16[4,192,768]{2,1,0:T(8,128)(2,1)S(1)}, bf16[4,192,768]{2,1,0:T(8,128)(2,1)S(1)}, u32[]{:S(2)}, u32[]{:S(2)}) collective-permute-start(bf16[4,192,768]{2,1,0:T(8,128)(2,1)S(1)} %fusion.79), channel_id=1, source_target_pairs={{0,4},{4,0},{8,12},{12,8},{16,20},{20,16},{24,28},{28,24},{1,5},{5... | collective-permute-start | bytes 3538952 | tf_op jit(solution)/shard_map/ppermute | solution.py:23
  447.2 4.0 collective-permute-start.16
  447.8 9.9 %collective-permute-start.12 = (bf16[1,192,768]{2,1,0:T(8,128)(2,1)S(1)}, bf16[1,192,768]{2,1,0:T(8,128)(2,1)S(1)}, u32[]{:S(2)}, u32[]{:S(2)}) collective-permute-start(bf16[1,192,768]{2,1,0:T(8,128)(2,1)S(1)} %dynamic-slice_convert_fusion.4), channel_id=1, source_target_pairs={{0,16},{4,20},{8,24},{12,28},{16,0},{20,4},{24,8},{28,12},{1,17},{... | collective-permute-start | bytes 884744 | tf_op jit(solution)/shard_map/ppermute | solution.py:23
  450.5 21.5 %collective-permute-start.24 = (bf16[1,192,768]{2,1,0:T(8,128)(2,1)S(1)}, bf16[1,192,768]{2,1,0:T(8,128)(2,1)S(1)}, u32[]{:S(2)}, u32[]{:S(2)}) collective-permute-start(bf16[1,192,768]{2,1,0:T(8,128)(2,1)S(1)} %dynamic-slice_convert_fusion.2), channel_id=1, source_target_pairs={{0,16},{4,20},{8,24},{12,28},{16,0},{20,4},{24,8},{28,12},{1,17},{... | collective-permute-start | bytes 884744 | tf_op jit(solution)/shard_map/ppermute | solution.py:23
  451.3 7.8 %collective-permute-start.17 = (bf16[2,192,256]{2,1,0:T(8,128)(2,1)S(1)}, bf16[2,192,256]{2,1,0:T(8,128)(2,1)S(1)}, u32[]{:S(2)}, u32[]{:S(2)}) collective-permute-start(bf16[2,192,256]{2,1,0:T(8,128)(2,1)S(1)} %fusion.107), channel_id=1, source_target_pairs={{0,8},{4,12},{8,0},{12,4},{16,24},{20,28},{24,16},{28,20},{1,9},{5... | collective-permute-start | bytes 589832 | tf_op jit(solution)/shard_map/ppermute | solution.py:23
  453.2 17.2 %collective-permute-start.14 = (bf16[2,192,768]{2,1,0:T(8,128)(2,1)S(1)}, bf16[2,192,768]{2,1,0:T(8,128)(2,1)S(1)}, u32[]{:S(2)}, u32[]{:S(2)}) collective-permute-start(bf16[2,192,768]{2,1,0:T(8,128)(2,1)S(1)} %fusion.92), channel_id=1, source_target_pairs={{0,8},{4,12},{8,0},{12,4},{16,24},{20,28},{24,16},{28,20},{1,9},{5... | collective-permute-start | bytes 1769480 | tf_op jit(solution)/shard_map/ppermute | solution.py:23
  458.6 14.3 %copy-start.72 = (f32[1024]{0:T(1024)S(1)}, f32[1024]{0:T(1024)}, u32[]{:S(2)}) copy-start(f32[1024]{0:T(1024)} %get-tuple-element.125) | copy-start | bytes 12292
  458.6 14.3 %copy-start.73 = (f32[1024]{0:T(1024)S(1)}, f32[1024]{0:T(1024)}, u32[]{:S(2)}) copy-start(f32[1024]{0:T(1024)} %get-tuple-element.126) | copy-start | bytes 12292
  458.6 14.3 %copy-start.74 = (f32[1024]{0:T(1024)S(1)}, f32[1024]{0:T(1024)}, u32[]{:S(2)}) copy-start(f32[1024]{0:T(1024)} %get-tuple-element.127) | copy-start | bytes 12292
  459.9 13.7 %collective-permute-start.18 = (bf16[1,192,256]{2,1,0:T(8,128)(2,1)}, bf16[1,192,256]{2,1,0:T(8,128)(2,1)}, u32[]{:S(2)}, u32[]{:S(2)}) collective-permute-start(bf16[1,192,256]{2,1,0:T(8,128)(2,1)} %dynamic-slice_convert_fusion.6), channel_id=1, source_target_pairs={{0,16},{4,20},{8,24},{12,28},{16,0},{20,4},{24,8},{28,12},{1,17},{... | collective-permute-start | bytes 294920 | tf_op jit(solution)/shard_map/ppermute | solution.py:23
  470.5 7.7 %collective-permute-start.15 = (bf16[1,192,768]{2,1,0:T(8,128)(2,1)S(1)}, bf16[1,192,768]{2,1,0:T(8,128)(2,1)S(1)}, u32[]{:S(2)}, u32[]{:S(2)}) collective-permute-start(bf16[1,192,768]{2,1,0:T(8,128)(2,1)S(1)} %dynamic-slice_convert_fusion.3), channel_id=1, source_target_pairs={{0,16},{4,20},{8,24},{12,28},{16,0},{20,4},{24,8},{28,12},{1,17},{... | collective-permute-start | bytes 884744 | tf_op jit(solution)/shard_map/ppermute | solution.py:23
  475.3 17.4 %copy-start.85 = (f32[768]{0:T(1024)S(1)}, f32[768]{0:T(1024)}, u32[]{:S(2)}) copy-start(f32[768]{0:T(1024)} %get-tuple-element.163) | copy-start | bytes 9220
  475.3 17.4 %copy-start.87 = (f32[12]{0:T(128)S(1)}, f32[12]{0:T(128)}, u32[]{:S(2)}) copy-start(f32[12]{0:T(128)} %get-tuple-element.142) | copy-start | bytes 148
  475.3 17.4 %copy-start.88 = (f32[12]{0:T(128)S(1)}, f32[12]{0:T(128)}, u32[]{:S(2)}) copy-start(f32[12]{0:T(128)} %reduce_sum.233) | copy-start | bytes 148
  475.3 17.4 %copy-start.100 = (f32[12]{0:T(128)S(1)}, f32[12]{0:T(128)}, u32[]{:S(2)}) copy-start(f32[12]{0:T(128)} %fusion.125) | copy-start | bytes 148
  (91 other events, 520.6 us)
Sparse Core Ops, SparseCore 0:
  167.2 57.8 reduce-scatter.2
  256.3 49.2 all-reduce.3
  307.7 62.6 all-gather.2
  373.2 59.0 reduce-scatter.4
  438.7 63.7 all-gather.4
